TPU v7x, 32 devices: a whole 2x2x4 slice. The times are simulated.
32 devices in a mesh: wide: 8 (over y, x, core), narrow: 4 (over z).
Axes of the slice: x: 2, y: 2, z: 4, core: 2. Of those that a mesh axis runs over, the one named last changes fastest.
Arguments:
- tokens: bfloat16 [64, 128, 1120], P(('wide', 'narrow')), may hold values from -6 to 6
- lengths: int32 [64], P(('wide', 'narrow')), may hold values from 1 to 128, 5120 in all
- ln1_gain: bfloat16 [1120], P('narrow'), may hold values from 0.5 to 1.5
- ln1_bias: bfloat16 [1120], P('narrow'), may hold values from -1 to 1
- w_qkv: bfloat16 [1120, 3360], P('narrow'), may hold values from -0.1875 to 0.1875
- w_out: bfloat16 [1120, 1120], P('narrow'), may hold values from -0.5 to 0.5
- ln2_gain: bfloat16 [1120], P('narrow'), may hold values from 0.5 to 1.5
- ln2_bias: bfloat16 [1120], P('narrow'), may hold values from -1 to 1
- w_fc: bfloat16 [1120, 4480], P('narrow'), may hold values from -0.1875 to 0.1875
- w_proj: bfloat16 [4480, 1120], P('narrow'), may hold values from -0.09375 to 0.09375
- cotangent: bfloat16 [64, 128, 1120], P(('wide', 'narrow')), may hold values from -6 to 6
Outputs:
- result: bfloat16 [64, 128, 1120], P(('wide', 'narrow'))
- grad_tokens: bfloat16 [64, 128, 1120], P(('wide', 'narrow'))
- grad_ln1_gain: float32 [1120], P('narrow')
- grad_ln1_bias: float32 [1120], P('narrow')
- grad_w_qkv: float32 [1120, 3360], P('narrow')
- grad_w_out: float32 [1120, 1120], P('narrow')
- grad_ln2_gain: float32 [1120], P('narrow')
- grad_ln2_bias: float32 [1120], P('narrow')
- grad_w_fc: float32 [1120, 4480], P('narrow')
- grad_w_proj: float32 [4480, 1120], P('narrow')
All inputs are finite; a program needn't handle non-finite values. No bound on the sum of `lengths` on one device may be relied on, other than what follows from the above.
Results may differ from a plain program's by a relative error of at most 0.015.
Values may be sent and summed in bfloat16 or wider, within the bound.
A program may use at most 256 MiB of HBM per device.

v0:
```python
from functools import partial
import jax
import jax.numpy as jnp
from jax import lax
from jax.sharding import PartitionSpec as P

HEADS = 20
EPS = 1e-05
MASKED = -1e30


def layer_norm(in_rows, gain_vec, shift_vec):
    row_mean = jnp.mean(in_rows, axis=-1, keepdims=True)
    centered = in_rows - row_mean
    inv_std = lax.rsqrt(jnp.mean(centered * centered, axis=-1, keepdims=True) + EPS)
    normed = centered * inv_std
    return (normed * gain_vec + shift_vec, normed, inv_std)


def norm_grad(grad_rows, gain_vec, normed, inv_std):
    scaled = grad_rows * gain_vec
    return inv_std * (
        scaled
        - jnp.mean(scaled, axis=-1, keepdims=True)
        - normed * jnp.mean(scaled * normed, axis=-1, keepdims=True)
    )


def inner_rows(left, right):
    return lax.dot_general(
        left, right, (((0,), (0,)), ((), ())), preferred_element_type=jnp.float32
    )


def times_trans(left, right):
    return lax.dot_general(
        left, right, (((1,), (1,)), ((), ())), preferred_element_type=jnp.float32
    )


def attn_scores(queries, key_rows, length):
    seq_len = queries.shape[0]
    head_size = queries.shape[2]
    scores = jnp.einsum(
        "qhd,khd->hqk", queries, key_rows, preferred_element_type=jnp.float32
    ) * head_size ** (-0.5)
    query_pos = lax.broadcasted_iota(jnp.int32, (seq_len, seq_len), 0)
    key_pos = lax.broadcasted_iota(jnp.int32, (seq_len, seq_len), 1)
    allowed = (key_pos <= query_pos) & (key_pos < length)
    return jnp.where(allowed[None], scores, MASKED)


def forward_cell(in_rows, length, weights):
    gain_one, shift_one, weight_qkv, weight_out, gain_two, shift_two, weight_fc, weight_proj = (
        weights
    )
    seq_len, model_width = in_rows.shape
    head_size = model_width // HEADS
    first_norm, normed_one, inv_one = layer_norm(
        in_rows, gain_one.astype(jnp.float32), shift_one.astype(jnp.float32)
    )
    first_low = first_norm.astype(jnp.bfloat16)
    projected = jnp.dot(first_low, weight_qkv, preferred_element_type=jnp.float32)
    queries = projected[:, :model_width].astype(jnp.bfloat16).reshape(seq_len, HEADS, head_size)
    key_rows = (
        projected[:, model_width : 2 * model_width]
        .astype(jnp.bfloat16)
        .reshape(seq_len, HEADS, head_size)
    )
    value_rows = (
        projected[:, 2 * model_width :].astype(jnp.bfloat16).reshape(seq_len, HEADS, head_size)
    )
    scores = attn_scores(queries, key_rows, length)
    row_max = jnp.max(scores, axis=-1, keepdims=True)
    exp_scores = jnp.exp(scores - row_max)
    row_total = jnp.sum(exp_scores, axis=-1, keepdims=True)
    attn_prob = exp_scores / row_total
    log_total = row_max + jnp.log(row_total)
    heads_out = jnp.einsum(
        "hqk,khd->qhd",
        attn_prob.astype(jnp.bfloat16),
        value_rows,
        preferred_element_type=jnp.float32,
    )
    attended = heads_out.reshape(seq_len, model_width).astype(jnp.bfloat16)
    mixed_rows = in_rows + jnp.dot(attended, weight_out, preferred_element_type=jnp.float32)
    second_norm, normed_two, inv_two = layer_norm(
        mixed_rows, gain_two.astype(jnp.float32), shift_two.astype(jnp.float32)
    )
    second_low = second_norm.astype(jnp.bfloat16)
    pre_act = jnp.dot(second_low, weight_fc, preferred_element_type=jnp.float32)
    gelu_out = jax.nn.gelu(pre_act, approximate=True).astype(jnp.bfloat16)
    result = mixed_rows + jnp.dot(gelu_out, weight_proj, preferred_element_type=jnp.float32)
    saved_acts = (
        normed_one,
        inv_one,
        first_low,
        queries,
        key_rows,
        value_rows,
        log_total,
        attended,
        normed_two,
        inv_two,
        second_low,
        pre_act,
        gelu_out,
    )
    return (result, saved_acts)


def backward_cell(grad_rows, length, saved_acts, weights):
    gain_one, shift_one, weight_qkv, weight_out, gain_two, shift_two, weight_fc, weight_proj = (
        weights
    )
    (
        normed_one,
        inv_one,
        first_low,
        queries,
        key_rows,
        value_rows,
        log_total,
        attended,
        normed_two,
        inv_two,
        second_low,
        pre_act,
        gelu_out,
    ) = saved_acts
    seq_len, model_width = grad_rows.shape
    head_size = model_width // HEADS
    grad_low = grad_rows.astype(jnp.bfloat16)
    grad_wproj = inner_rows(gelu_out, grad_low)
    grad_gelu = times_trans(grad_low, weight_proj)
    unused, gelu_pull = jax.vjp(partial(jax.nn.gelu, approximate=True), pre_act)
    grad_pre = gelu_pull(grad_gelu)[0].astype(jnp.bfloat16)
    grad_wfc = inner_rows(second_low, grad_pre)
    grad_second = times_trans(grad_pre, weight_fc)
    grad_gain_two = jnp.sum(grad_second * normed_two, axis=0)
    grad_shift_two = jnp.sum(grad_second, axis=0)
    grad_mixed = grad_rows + norm_grad(
        grad_second, gain_two.astype(jnp.float32), normed_two, inv_two
    )
    mixed_low = grad_mixed.astype(jnp.bfloat16)
    grad_wout = inner_rows(attended, mixed_low)
    grad_attended = (
        times_trans(mixed_low, weight_out).astype(jnp.bfloat16).reshape(seq_len, HEADS, head_size)
    )
    scores = attn_scores(queries, key_rows, length)
    attn_prob = jnp.exp(scores - log_total)
    grad_value = jnp.einsum(
        "hqk,qhd->khd",
        attn_prob.astype(jnp.bfloat16),
        grad_attended,
        preferred_element_type=jnp.float32,
    )
    grad_prob = jnp.einsum(
        "qhd,khd->hqk", grad_attended, value_rows, preferred_element_type=jnp.float32
    )
    grad_scores = attn_prob * (grad_prob - jnp.sum(attn_prob * grad_prob, axis=-1, keepdims=True))
    grad_scores = grad_scores.astype(jnp.bfloat16)
    scale_factor = head_size ** (-0.5)
    grad_query = (
        jnp.einsum("hqk,khd->qhd", grad_scores, key_rows, preferred_element_type=jnp.float32)
        * scale_factor
    )
    grad_key = (
        jnp.einsum("hqk,qhd->khd", grad_scores, queries, preferred_element_type=jnp.float32)
        * scale_factor
    )
    grad_proj_in = jnp.concatenate(
        [
            grad_query.reshape(seq_len, model_width),
            grad_key.reshape(seq_len, model_width),
            grad_value.reshape(seq_len, model_width),
        ],
        axis=1,
    ).astype(jnp.bfloat16)
    grad_wqkv = inner_rows(first_low, grad_proj_in)
    grad_first = times_trans(grad_proj_in, weight_qkv)
    grad_gain_one = jnp.sum(grad_first * normed_one, axis=0)
    grad_shift_one = jnp.sum(grad_first, axis=0)
    grad_input = grad_mixed + norm_grad(
        grad_first, gain_one.astype(jnp.float32), normed_one, inv_one
    )
    grads = (
        grad_gain_one,
        grad_shift_one,
        grad_wqkv,
        grad_wout,
        grad_gain_two,
        grad_shift_two,
        grad_wfc,
        grad_wproj,
    )
    return (grads, grad_input)


def shards(
    tokens, lengths, ln1_gain, ln1_bias, w_qkv, w_out, ln2_gain, ln2_bias, w_fc, w_proj, cotangent
):
    outputs = []
    input_grads = []
    running = None
    held = None
    held = (
        lax.all_gather(ln1_gain, "narrow", axis=0, tiled=True),
        lax.all_gather(ln1_bias, "narrow", axis=0, tiled=True),
        lax.all_gather(w_qkv, "narrow", axis=0, tiled=True),
        lax.all_gather(w_out, "narrow", axis=0, tiled=True),
        lax.all_gather(ln2_gain, "narrow", axis=0, tiled=True),
        lax.all_gather(ln2_bias, "narrow", axis=0, tiled=True),
        lax.all_gather(w_fc, "narrow", axis=0, tiled=True),
        lax.all_gather(w_proj, "narrow", axis=0, tiled=True),
    )
    for micro_step in range(tokens.shape[0]):
        in_rows = tokens[micro_step].astype(jnp.float32)
        result, saved_acts = forward_cell(in_rows, lengths[micro_step], held)
        grads, grad_input = backward_cell(
            cotangent[micro_step].astype(jnp.float32), lengths[micro_step], saved_acts, held
        )
        running = grads if running is None else jax.tree.map(jnp.add, running, grads)
        outputs.append(result.astype(jnp.bfloat16))
        input_grads.append(grad_input.astype(jnp.bfloat16))
    totals = []
    for grad in running:
        part = lax.psum_scatter(
            grad.astype(jnp.bfloat16), "narrow", scatter_dimension=0, tiled=True
        )
        if part.ndim == 2:
            part = lax.psum(part, "wide").astype(jnp.float32)
        else:
            part = lax.psum(part.astype(jnp.float32), "wide")
        totals.append(part)
    return (
        jnp.stack(outputs),
        jnp.stack(input_grads),
        totals[0],
        totals[1],
        totals[2],
        totals[3],
        totals[4],
        totals[5],
        totals[6],
        totals[7],
    )


def solution(mesh):
    placed = (
        P(("wide", "narrow"), None, None),
        P(("wide", "narrow")),
        P("narrow"),
        P("narrow"),
        P("narrow", None),
        P("narrow", None),
        P("narrow"),
        P("narrow"),
        P("narrow", None),
        P("narrow", None),
        P(("wide", "narrow"), None, None),
    )
    return jax.shard_map(
        shards,
        mesh=mesh,
        in_specs=placed,
        out_specs=(
            P(("wide", "narrow"), None, None),
            P(("wide", "narrow"), None, None),
            P("narrow"),
            P("narrow"),
            P("narrow", None),
            P("narrow", None),
            P("narrow"),
            P("narrow"),
            P("narrow", None),
            P("narrow", None),
        ),
        check_vma=False,
    )
```

profile of v0, /device:TPU:0, one launch (start us, length us, event | category | flops | bytes accessed | tf_op | source)
XLA Modules:
  0.0 1292.5 jit_solution(16745767182800808506)
XLA Ops:
  7.2 0.7 all-gather.5.cloned.1.call-update
  8.0 0.7 all-gather.7.cloned.1.call-update
  8.8 0.7 all-gather.9.cloned.1.call-update
  10.1 0.6 fusion.108
  12.4 21.1 %all-reduce.14 = (bf16[1120]{0:T(1024)(128)(2,1)S(1)}, bf16[1120]{0:T(1024)(128)(2,1)S(1)}, bf16[1120]{0:T(1024)(128)(2,1)S(1)}, bf16[1120]{0:T(1024)(128)(2,1)S(1)}) all-reduce(bf16[1120]{0:T(1024)(128)(2,1)S(1)} %dynamic-update-slice.1, bf16[1120]{0:T(1024)(128)(2,1)S(1)} %dynamic-update-slice, ...), channel_id=1, replica_groups=mesh['wide'=8,'narrow'=4] {'narrow'}, use_global_device_ids=true, to_apply=%add.1 | all-reduce | flops 4480 | bytes 17920
  33.5 0.6 fusion.109
  34.1 0.6 iota_compare_fusion.2
  34.8 0.7 iota_compare_fusion.1
  36.0 115.5 %all-gather.5.cloned.1.call-done = bf16[1120,3360]{1,0:T(8,128)(2,1)} async-done(((bf16[280,3360]{1,0:T(8,128)(2,1)}), bf16[1120,3360]{1,0:T(8,128)(2,1)}) %all-gather.5.cloned.1.call-update) | async-done | bytes 7526416 | tf_op jit(solution)/shard_map/all_gather | solution.py:210
  151.5 6.6 convolution_convert_fusion.1
  158.8 0.8 copy-done.2
  160.1 45.3 %all-gather.7.cloned.1.call-done = bf16[1120,1120]{1,0:T(8,128)(2,1)} async-done(((bf16[280,1120]{1,0:T(8,128)(2,1)}), bf16[1120,1120]{1,0:T(8,128)(2,1)}) %all-gather.7.cloned.1.call-update) | async-done | bytes 2508816 | tf_op jit(solution)/shard_map/all_gather | solution.py:211
  205.3 2.8 fusion.113
  208.4 6.6 convolution_convert_fusion
  216.5 1.5 copy-done.1
  218.2 1.1 fusion.111
  219.4 0.8 copy-done.8
  220.9 161.4 %all-gather.9.cloned.1.call-done = bf16[1120,4480]{1,0:T(8,128)(2,1)} async-done(((bf16[280,4480]{1,0:T(8,128)(2,1)}), bf16[1120,4480]{1,0:T(8,128)(2,1)}) %all-gather.9.cloned.1.call-update) | async-done | bytes 10035216 | tf_op jit(solution)/shard_map/all_gather | solution.py:214
  382.2 7.6 fusion.105
  389.9 173.2 %all-gather.11.cloned.1.call-done = bf16[4480,1120]{1,0:T(8,128)(2,1)} async-done(((bf16[1120,1120]{1,0:T(8,128)(2,1)}), bf16[4480,1120]{1,0:T(8,128)(2,1)}) %all-gather.11.cloned.1.call-update) | async-done | bytes 10035216 | tf_op jit(solution)/shard_map/all_gather | solution.py:215
  563.1 8.1 fusion.21
  571.3 1.0 copy-done.28
  572.3 2.8 fusion.114
  575.1 1.9 fusion.104
  577.0 8.1 fusion.14
  585.1 3.9 multiply_reduce_fusion.3
  590.0 0.8 fusion.90
  591.0 2.3 fusion.3
  593.4 2.0 convolution_convert_fusion.2
  596.3 0.6 copy-done.35
  596.9 0.6 fusion.27
  597.9 0.8 convolution_convert_fusion.3
  598.7 0.6 copy-done.3
  600.2 0.6 copy-done.31
  600.8 0.6 fusion.25
  601.7 0.6 convolution_convert_fusion.5
  602.3 0.6 convolution_convert_fusion.4
  602.9 7.7 fusion.69
  610.7 8.7 fusion.2
  619.5 1.2 copy-done.27
  620.6 8.7 fusion.103
  629.4 11.7 fusion.1
  641.2 1.6 copy-done.18
  642.8 9.2 fusion.78
  652.0 14.9 %fusion = bf16[4480,1120]{1,0:T(8,128)(2,1)} fusion(f32[4480,1120]{1,0:T(8,128)} %fusion.78, bf16[2,128,1120]{1,2,0:T(8,128)(2,1)S(1)} %copy-done.38, f32[128,4480]{1,0:T(8,128)} %fusion.105), kind=kOutput, calls=%fused_computation.3 | convolution fusion | flops 1299701760 | bytes 32686080 | tf_op jit(solution)/shard_map/dot_general | solution.py:30
  667.8 1.5 add_convert_fusion.3
  669.3 1.3 add_convert_fusion.2
  670.7 5.7 fusion.68
  676.4 3.7 fusion.66
  680.1 21.4 %all-reduce.13 = (bf16[1120]{0:T(1024)(128)(2,1)S(1)}, bf16[1120]{0:T(1024)(128)(2,1)S(1)}, bf16[1120]{0:T(1024)(128)(2,1)S(1)}, bf16[1120]{0:T(1024)(128)(2,1)S(1)}) all-reduce(bf16[1120]{0:T(1024)(128)(2,1)S(1)} %add_convert_fusion.5, ...), channel_id=2, replica_groups=mesh['wide'=8,'narrow'=4] {'narrow'}, use_global_device_ids=true, to_apply=%region_24.25.clone | all-reduce | flops 4480 | bytes 17920
  701.6 78.5 %reduce-scatter.13.cloned.1.call-done = bf16[280,3360]{1,0:T(8,128)(2,1)} async-done(((bf16[1120,3360]{1,0:T(8,128)(2,1)}), bf16[280,3360]{1,0:T(8,128)(2,1)}) %reduce-scatter.13.cloned.1.call-update) | async-done | bytes 1881616
  780.2 187.7 %reduce-scatter.17.cloned.1.call-done = bf16[280,4480]{1,0:T(8,128)(2,1)} async-done(((bf16[1120,4480]{1,0:T(8,128)(2,1)}), bf16[280,4480]{1,0:T(8,128)(2,1)}) %reduce-scatter.17.cloned.1.call-update) | async-done | bytes 2508816
  967.8 182.3 %reduce-scatter.11.cloned.1.call-done = bf16[1120,1120]{1,0:T(8,128)(2,1)} async-done(((bf16[4480,1120]{1,0:T(8,128)(2,1)}), bf16[1120,1120]{1,0:T(8,128)(2,1)}) %reduce-scatter.11.cloned.1.call-update) | async-done | bytes 2508816 | tf_op jit(solution)/shard_map/reduce_scatter | solution.py:228
  1150.3 14.7 %all-reduce.11 = (f32[280]{0:T(512)}, f32[280]{0:T(512)}, f32[280]{0:T(512)}, f32[280]{0:T(512)}) all-reduce(f32[280]{0:T(512)S(1)} %dynamic-slice_convert_fusion.3, f32[280]{0:T(512)S(1)} %dynamic-slice_convert_fusion.2, f32[280]{0:T(512)S(1)} %dynamic-slice_convert_fusion.1, ...), channel_id=1, replica_groups=mesh['wide'=8,'narrow'=4] {'wide'}, use_global_device_ids=true, to_apply=%region_25.26 | all-reduce | flops 1120 | bytes 8960 | tf_op jit(solution)/shard_map/psum | solution.py:234
  1165.1 8.3 fusion.6
  1173.6 8.4 fusion.7
  1182.0 0.9 pad_maximum_fusion.2
  1183.3 0.9 pad_maximum_fusion.3
  1184.2 90.5 %all-reduce.17.cloned.1.call-done = (bf16[280,3360]{1,0:T(8,128)(2,1)}, bf16[280,1120]{1,0:T(8,128)(2,1)}, bf16[280,4480]{1,0:T(8,128)(2,1)}, bf16[1120,1120]{1,0:T(8,128)(2,1)}) async-done(((bf16[280,3360]{1,0:T(8,128)(2,1)}, bf16[280,1120]{1,0:T(8,128)(2,1)}, bf16[280,4480]{1,0:T(8,128)(2,1)}, bf16[1120,1120]{1,0:T(8,128)(2,1)}), (bf16[280,3360]{1,0:T(8,128)(2,1)}, bf16[280,1120]{1,0:T(8,128)(2,1)}, ...) | async-done | bytes 7526416 | tf_op jit(solution)/shard_map/psum | solution.py:232
  1274.7 2.4 convert_element_type.225
  1277.1 2.2 convert_element_type.223
  1279.3 0.8 copy-done.36
  1280.0 2.6 convert_element_type.231
  1282.8 2.7 convert_element_type.233
  (238 shorter events, 10.8 us)
Async XLA Ops:
  7.2 144.3 %all-gather.5.cloned.1.call-start = ((), (), s32[]{:S(2)}) async-start(), calls=%async_computation.4 | async-start | bytes 9676800 | tf_op jit(solution)/shard_map/all_gather | solution.py:210
  7.9 197.4 %all-gather.7.cloned.1.call-start = ((), (), s32[]{:S(2)}) async-start(), calls=%async_computation.5 | async-start | bytes 3225600 | tf_op jit(solution)/shard_map/all_gather | solution.py:211
  8.7 2.9 copy-start.78
  8.7 3.2 copy-start.79
  8.7 3.4 copy-start.80
  8.7 24.8 %copy-start.76 = (s32[2]{0:T(128)S(1)}, s32[2]{0:T(128)}, u32[]{:S(2)}) copy-start(s32[2]{0:T(128)} %param.12) | copy-start | bytes 28
  8.7 26.7 %copy-start.12 = (bf16[2,128,1120]{1,2,0:T(8,128)(2,1)S(1)}, bf16[2,128,1120]{1,2,0:T(8,128)(2,1)}, u32[]{:S(2)}) copy-start(bf16[2,128,1120]{1,2,0:T(8,128)(2,1)} %param.11) | copy-start | bytes 1720324
  8.7 373.5 %all-gather.9.cloned.1.call-start = ((), (), s32[]{:S(2)}) async-start(), calls=%async_computation.6 | async-start | bytes 12544000 | tf_op jit(solution)/shard_map/all_gather | solution.py:214
  9.5 553.6 %all-gather.11.cloned.1.call-start = ((), (), s32[]{:S(2)}) async-start(), calls=%async_computation.7 | async-start | bytes 12902400 | tf_op jit(solution)/shard_map/all_gather | solution.py:215
  10.0 691.6 %reduce-scatter.15.cloned.1.call-start = ((), (), s32[]{:S(2)}) async-start(), calls=%async_computation.10 | async-start | bytes 3225600
  35.6 172.8 %copy-start.67 = (f32[128]{0:T(128)}, f32[128]{0:T(128)S(1)}, u32[]{:S(2)}) copy-start(f32[128]{0:T(128)S(1)} %get-tuple-element.80) | copy-start | bytes 1540
  35.6 567.3 %copy-start.60 = (f32[128]{0:T(128)}, f32[128]{0:T(128)S(1)}, u32[]{:S(2)}) copy-start(f32[128]{0:T(128)S(1)} %get-tuple-element.81) | copy-start | bytes 1540
  35.8 567.1 %copy-start.63 = (f32[128]{0:T(128)}, f32[128]{0:T(128)S(1)}, u32[]{:S(2)}) copy-start(f32[128]{0:T(128)S(1)} %add_rsqrt_fusion.3) | copy-start | bytes 1540
  35.8 172.6 %copy-start.71 = (f32[128]{0:T(128)}, f32[128]{0:T(128)S(1)}, u32[]{:S(2)}) copy-start(f32[128]{0:T(128)S(1)} %add_rsqrt_fusion.1) | copy-start | bytes 1540
  160.1 48.1 %copy-start.53 = (bf16[20,56,128]{2,1,0:T(8,128)(2,1)}, bf16[20,56,128]{2,1,0:T(8,128)(2,1)S(1)}, u32[]{:S(2)}) copy-start(bf16[20,56,128]{2,1,0:T(8,128)(2,1)S(1)} %convolution_convert_fusion.7) | copy-start | bytes 860164
  208.2 411.3 %copy-start.6 = (f32[128,1120]{0,1:T(8,128)}, f32[128,1120]{0,1:T(8,128)S(1)}, u32[]{:S(2)}) copy-start(f32[128,1120]{0,1:T(8,128)S(1)} %get-tuple-element.73) | copy-start | bytes 1720324
  216.5 3.8 copy-start.55
  563.1 9.2 copy-start
  576.9 8.2 copy-start.17
  576.9 8.2 copy-start.9
  577.0 8.2 copy-start.66
  585.1 3.9 copy-start.26
  593.3 186.8 %reduce-scatter.13.cloned.1.call-start = ((), (), s32[]{:S(2)}) async-start(), calls=%async_computation.9 | async-start | bytes 9676800
  597.5 13.2 %copy-start.40 = (bf16[20,56,128]{2,1,0:T(8,128)(2,1)}, bf16[20,56,128]{2,1,0:T(8,128)(2,1)S(1)}, u32[]{:S(2)}) copy-start(bf16[20,56,128]{2,1,0:T(8,128)(2,1)S(1)} %fusion.27) | copy-start | bytes 860164
  597.8 12.9 copy-start.41
  601.7 9.0 copy-start.44
  602.3 8.4 copy-start.46
  602.9 7.8 copy-start.48
  602.9 7.8 copy-start.68
  602.9 7.8 copy-start.72
  619.4 10.0 copy-start.10
  619.4 348.4 %reduce-scatter.17.cloned.1.call-start = ((), (), s32[]{:S(2)}) async-start(), calls=%async_computation.11 | async-start | bytes 12544000
  641.1 509.0 %reduce-scatter.11.cloned.1.call-start = ((), (), s32[]{:S(2)}) async-start(), calls=%async_computation.8 | async-start | bytes 12902400 | tf_op jit(solution)/shard_map/reduce_scatter | solution.py:228
  666.9 9.4 slice-start
  666.9 607.8 %all-reduce.17.cloned.1.call-start = ((), (), s32[]{:S(2)}) async-start(), calls=%async_computation.12 | async-start | bytes 15339520 | tf_op jit(solution)/shard_map/psum | solution.py:232
  670.6 5.7 slice-start.1
  670.6 5.7 copy-start.15
  670.6 5.8 copy-start.43
  670.6 5.8 copy-start.45
  670.6 5.8 copy-start.47
  670.6 5.8 copy-start.61
  670.6 5.8 copy-start.64
  670.6 5.8 copy-start.69
  670.7 5.8 copy-start.73
  676.4 3.7 copy-start.57
  1150.1 14.9 %copy-start.84 = (f32[128]{0:T(128)S(1)}, f32[128]{0:T(128)}, u32[]{:S(2)}) copy-start(f32[128]{0:T(128)} %get-tuple-element.17) | copy-start | bytes 1540
  1150.1 14.9 %copy-start.83 = (f32[128]{0:T(128)S(1)}, f32[128]{0:T(128)}, u32[]{:S(2)}) copy-start(f32[128]{0:T(128)} %get-tuple-element.18) | copy-start | bytes 1540
  1150.1 14.9 %copy-start.82 = (f32[128]{0:T(128)S(1)}, f32[128]{0:T(128)}, u32[]{:S(2)}) copy-start(f32[128]{0:T(128)} %get-tuple-element.20) | copy-start | bytes 1540
  1150.1 15.0 %copy-start.81 = (f32[128]{0:T(128)S(1)}, f32[128]{0:T(128)}, u32[]{:S(2)}) copy-start(f32[128]{0:T(128)} %get-tuple-element.21) | copy-start | bytes 1540
  1150.1 15.0 %copy-start.11 = (f32[128,1120]{0,1:T(8,128)S(1)}, f32[128,1120]{0,1:T(8,128)}, u32[]{:S(2)}) copy-start(f32[128,1120]{0,1:T(8,128)} %copy-done.8) | copy-start | bytes 1720324
  1150.1 15.0 %copy-start.20 = (f32[128,4480]{1,0:T(8,128)S(1)}, f32[128,4480]{1,0:T(8,128)}, u32[]{:S(2)}) copy-start(f32[128,4480]{1,0:T(8,128)} %fusion.105) | copy-start | bytes 6881284
  1165.1 8.4 copy-start.7
  1165.1 8.4 copy-start.19
  1173.5 9.4 copy-start.16
  1173.5 9.4 copy-start.23
  1173.5 9.4 copy-start.25
  1173.5 9.4 copy-start.58
  1173.5 9.4 copy-start.59
  1173.5 9.4 copy-start.62
  1173.6 9.4 copy-start.65
  1173.6 9.4 copy-start.70
  1173.6 9.4 copy-start.74
  1277.1 2.9 copy-start.36
  1280.0 2.8 copy-start.29
  (32 other events, 48.1 us)
Sparse Core Ops, SparseCore 0:
  9.6 141.9 all-gather.4
  153.1 52.2 all-gather.6
  206.9 175.2 all-gather.8
  383.7 179.3 all-gather.10
  593.5 49.2 reduce-scatter.14
  644.9 135.2 reduce-scatter.12
  782.5 185.2 reduce-scatter.16
  970.2 179.8 reduce-scatter.10
  1153.9 120.8 all-reduce.16
where the time goes:
time: 1300 us; the launch traced here: 1290 us
  waiting for transfers between devices  1040 us (80%)
  matrix products  148 us (11%)
  blocking collectives  57.2 us (4%)
  other arithmetic  19.2 us (1%)
  between operations  17 us (1%)
  local copies, waits for them, and re-layouts  13.7 us (1%)
    unnamed x12, waiting for transfers between devices  269 us
    reduce_scatter x1, waiting for transfers between devices, shards(): lax.psum_scatter(grad.astype(jnp.bfloat16), 'narrow', scatter_dimension=0...  182 us
    all_gather x1, waiting for transfers between devices, shards(): lax.all_gather(w_proj, 'narrow', axis=0, tiled=True)  173 us
    all_gather x1, waiting for transfers between devices, shards(): lax.all_gather(w_fc, 'narrow', axis=0, tiled=True)  161 us
    all_gather x1, waiting for transfers between devices, shards(): lax.all_gather(w_qkv, 'narrow', axis=0, tiled=True)  116 us
    psum x1, waiting for transfers between devices, shards(): part = lax.psum(part, 'wide').astype(jnp.float32)  90.5 us
    dot_general x8, matrix products, inner_rows(): lax.dot_general(left, right, (((0,), (0,)), ((), ())), preferred_element_...  64.1 us
    all_gather x1, waiting for transfers between devices, shards(): lax.all_gather(w_out, 'narrow', axis=0, tiled=True)  45.3 us
  transfers between devices with their start and end apart: 9, of which 8 were waited for; matrix products, arithmetic and copies ran while one was open for 10% of the time, Pallas kernels for 0%

commit v1 on v0

--- a/solution.py
+++ b/solution.py
@@ -229,7 +229,12 @@
             grad.astype(jnp.bfloat16), "narrow", scatter_dimension=0, tiled=True
         )
         if part.ndim == 2:
-            part = lax.psum(part, "wide").astype(jnp.float32)
+
+            def load_local_data_over_axis(field):
+                work_now = jnp.sum(jax.lax.all_gather(field, "wide"), axis=0)
+                return work_now
+
+            part = load_local_data_over_axis(part).astype(jnp.float32)
         else:
             part = lax.psum(part.astype(jnp.float32), "wide")
         totals.append(part)

time: 1300 us -> 1520 us (1.17)
  waiting for transfers between devices: 1040 us -> 1220 us
  other arithmetic: 19.2 us -> 56.1 us
    all_gather x0 -> x4, waiting for transfers between devices: none -> 245 us  [load_local_data_over_axis(): work_now = jnp.sum(jax.lax.all_gather(field, 'wide'), axis=0)]
    psum x1 -> x0, waiting for transfers between devices: 90.5 us -> none  [shards(): part = lax.psum(part, 'wide').astype(jnp.float32)]
    reduce_sum x0 -> x4, other arithmetic: none -> 35.3 us  [load_local_data_over_axis(): work_now = jnp.sum(jax.lax.all_gather(field, 'wide'), axis=0)]
    unnamed x12 -> x15, waiting for transfers between devices: 269 us -> 303 us
  transfers between devices with their start and end apart: 9 -> 12, of which waited for: 8 -> 10; matrix products, arithmetic and copies ran while one was open for 10% -> 11% of each run, Pallas kernels for 0% -> 0%
where the time goes in v1:
time: 1520 us; the launch traced here: 1510 us
  waiting for transfers between devices  1220 us (80%)
  matrix products  149 us (10%)
  other arithmetic  56.1 us (4%)
  blocking collectives  53.7 us (4%)
  between operations  16.9 us (1%)
    unnamed x15, waiting for transfers between devices  303 us
    all_gather x4, waiting for transfers between devices, load_local_data_over_axis(): work_now = jnp.sum(jax.lax.all_gather(field, 'wide'), axis=0)  245 us
    reduce_scatter x1, waiting for transfers between devices, shards(): lax.psum_scatter(grad.astype(jnp.bfloat16), 'narrow', scatter_dimension=0...  181 us
    all_gather x1, waiting for transfers between devices, shards(): lax.all_gather(w_proj, 'narrow', axis=0, tiled=True)  173 us
    all_gather x1, waiting for transfers between devices, shards(): lax.all_gather(w_fc, 'narrow', axis=0, tiled=True)  161 us
    all_gather x1, waiting for transfers between devices, shards(): lax.all_gather(w_qkv, 'narrow', axis=0, tiled=True)  116 us
    dot_general x8, matrix products, inner_rows(): lax.dot_general(left, right, (((0,), (0,)), ((), ())), preferred_element_...  64.7 us
    all_gather x1, waiting for transfers between devices, shards(): lax.all_gather(w_out, 'narrow', axis=0, tiled=True)  45.3 us
  transfers between devices with their start and end apart: 12, of which 10 were waited for; matrix products, arithmetic and copies ran while one was open for 11% of the time, Pallas kernels for 0%

profile of v1, /device:TPU:0, one launch (start us, length us, event | category | flops | bytes accessed | tf_op | source)
XLA Modules:
  0.0 1514.1 jit_solution(3001389140364785348)
XLA Ops:
  7.2 0.7 all-gather.13.cloned.1.call-update
  8.0 0.7 all-gather.15.cloned.1.call-update
  8.8 0.7 all-gather.17.cloned.1.call-update
  12.4 21.1 %all-reduce.13 = (bf16[1120]{0:T(1024)(128)(2,1)S(1)}, bf16[1120]{0:T(1024)(128)(2,1)S(1)}, bf16[1120]{0:T(1024)(128)(2,1)S(1)}, bf16[1120]{0:T(1024)(128)(2,1)S(1)}) all-reduce(bf16[1120]{0:T(1024)(128)(2,1)S(1)} %dynamic-update-slice.1, bf16[1120]{0:T(1024)(128)(2,1)S(1)} %dynamic-update-slice, ...), channel_id=1, replica_groups=mesh['wide'=8,'narrow'=4] {'narrow'}, use_global_device_ids=true, to_apply=%add.1 | all-reduce | flops 4480 | bytes 17920
  34.1 0.6 iota_compare_fusion.2
  34.8 0.7 iota_compare_fusion.1
  36.0 115.5 %all-gather.13.cloned.1.call-done = bf16[1120,3360]{1,0:T(8,128)(2,1)} async-done(((bf16[280,3360]{1,0:T(8,128)(2,1)}), bf16[1120,3360]{1,0:T(8,128)(2,1)}) %all-gather.13.cloned.1.call-update) | async-done | bytes 7526416 | tf_op jit(solution)/shard_map/all_gather | solution.py:210
  151.5 6.6 convolution_convert_fusion.1
  158.8 0.9 copy-done.2
  160.1 45.3 %all-gather.15.cloned.1.call-done = bf16[1120,1120]{1,0:T(8,128)(2,1)} async-done(((bf16[280,1120]{1,0:T(8,128)(2,1)}), bf16[1120,1120]{1,0:T(8,128)(2,1)}) %all-gather.15.cloned.1.call-update) | async-done | bytes 2508816 | tf_op jit(solution)/shard_map/all_gather | solution.py:211
  205.3 2.8 fusion.113
  208.4 6.6 convolution_convert_fusion
  216.6 1.5 copy-done.1
  218.2 1.1 fusion.111
  219.4 0.8 copy-done.8
  220.9 161.4 %all-gather.17.cloned.1.call-done = bf16[1120,4480]{1,0:T(8,128)(2,1)} async-done(((bf16[280,4480]{1,0:T(8,128)(2,1)}), bf16[1120,4480]{1,0:T(8,128)(2,1)}) %all-gather.17.cloned.1.call-update) | async-done | bytes 10035216 | tf_op jit(solution)/shard_map/all_gather | solution.py:214
  382.2 7.4 fusion.105
  389.7 173.4 %all-gather.19.cloned.1.call-done = bf16[4480,1120]{1,0:T(8,128)(2,1)} async-done(((bf16[1120,1120]{1,0:T(8,128)(2,1)}), bf16[4480,1120]{1,0:T(8,128)(2,1)}) %all-gather.19.cloned.1.call-update) | async-done | bytes 10035216 | tf_op jit(solution)/shard_map/all_gather | solution.py:215
  563.1 8.1 fusion.21
  571.3 1.0 copy-done.26
  572.3 2.8 fusion.114
  575.1 1.9 fusion.104
  577.0 8.1 fusion.14
  585.1 4.0 multiply_reduce_fusion.3
  590.1 0.8 fusion.90
  591.0 2.3 fusion.3
  593.5 2.0 convolution_convert_fusion.2
  597.9 0.8 convolution_convert_fusion.3
  603.0 7.7 fusion.69
  610.8 8.8 fusion.2
  619.7 1.2 copy-done.25
  620.8 9.0 fusion.103
  629.9 11.8 fusion.1
  641.7 1.6 copy-done.17
  643.4 9.5 fusion.78
  652.9 14.7 fusion
  667.8 0.7 all-gather.23.cloned.1.call-update
  668.5 111.2 %reduce-scatter.13.cloned.1.call-done = bf16[280,3360]{1,0:T(8,128)(2,1)} async-done(((bf16[1120,3360]{1,0:T(8,128)(2,1)}), bf16[280,3360]{1,0:T(8,128)(2,1)}) %reduce-scatter.13.cloned.1.call-update) | async-done | bytes 1881616
  779.8 188.9 %reduce-scatter.17.cloned.1.call-done = bf16[280,4480]{1,0:T(8,128)(2,1)} async-done(((bf16[1120,4480]{1,0:T(8,128)(2,1)}), bf16[280,4480]{1,0:T(8,128)(2,1)}) %reduce-scatter.17.cloned.1.call-update) | async-done | bytes 2508816
  968.7 181.0 %reduce-scatter.11.cloned.1.call-done = bf16[1120,1120]{1,0:T(8,128)(2,1)} async-done(((bf16[4480,1120]{1,0:T(8,128)(2,1)}), bf16[1120,1120]{1,0:T(8,128)(2,1)}) %reduce-scatter.11.cloned.1.call-update) | async-done | bytes 2508816 | tf_op jit(solution)/shard_map/reduce_scatter | solution.py:228
  1150.3 1.3 add_convert_fusion.3
  1151.6 1.3 add_convert_fusion.2
  1153.0 5.7 fusion.68
  1158.8 3.7 fusion.66
  1162.5 19.2 %all-reduce.12 = (bf16[1120]{0:T(1024)(128)(2,1)S(1)}, bf16[1120]{0:T(1024)(128)(2,1)S(1)}, bf16[1120]{0:T(1024)(128)(2,1)S(1)}, bf16[1120]{0:T(1024)(128)(2,1)S(1)}) all-reduce(bf16[1120]{0:T(1024)(128)(2,1)S(1)} %add_convert_fusion.5, ...), channel_id=6, replica_groups=mesh['wide'=8,'narrow'=4] {'narrow'}, use_global_device_ids=true, to_apply=%region_24.25.clone | all-reduce | flops 4480 | bytes 17920
  1182.0 13.4 all-reduce.11
  1196.0 0.7 broadcast_multiply_fusion
  1196.7 0.7 broadcast_multiply_fusion.1
  1197.4 0.6 broadcast_multiply_fusion.5
  1198.0 9.4 fusion.6
  1207.5 8.2 fusion.7
  1215.8 0.9 pad_maximum_fusion.2
  1217.1 0.9 pad_maximum_fusion.3
  1218.0 3.5 reduce_sum.325
  1221.5 1.1 convert_element_type.233
  1222.6 57.1 %all-gather.21.cloned.1.call-done = bf16[2240,3360]{1,0:T(8,128)(2,1)} async-done(((bf16[280,3360]{1,0:T(8,128)(2,1)}), bf16[2240,3360]{1,0:T(8,128)(2,1)}) %all-gather.21.cloned.1.call-update) | async-done | bytes 15052816 | tf_op jit(solution)/shard_map/all_gather | solution.py:234
  1279.7 8.6 reduce_sum.324
  1288.3 2.4 convert_element_type.231
  1290.7 94.6 %all-gather.25.cloned.1.call-done = bf16[2240,4480]{1,0:T(8,128)(2,1)} async-done(((bf16[280,4480]{1,0:T(8,128)(2,1)}), bf16[2240,4480]{1,0:T(8,128)(2,1)}) %all-gather.25.cloned.1.call-update) | async-done | bytes 20070416 | tf_op jit(solution)/shard_map/all_gather | solution.py:234
  1385.3 11.9 reduce_sum.330
  1397.2 2.8 convert_element_type.239
  1400.0 93.2 %all-gather.27.cloned.1.call-done = bf16[8960,1120]{1,0:T(8,128)(2,1)} async-done(((bf16[1120,1120]{1,0:T(8,128)(2,1)}), bf16[8960,1120]{1,0:T(8,128)(2,1)}) %all-gather.27.cloned.1.call-update) | async-done | bytes 20070416 | tf_op jit(solution)/shard_map/all_gather | solution.py:234
  1493.1 11.3 reduce_sum.331
  1504.4 2.7 convert_element_type.241
  (233 shorter events, 16.5 us)
Async XLA Ops:
  7.2 144.3 %all-gather.13.cloned.1.call-start = ((), (), s32[]{:S(2)}) async-start(), calls=%async_computation.4 | async-start | bytes 9676800 | tf_op jit(solution)/shard_map/all_gather | solution.py:210
  7.9 197.4 %all-gather.15.cloned.1.call-start = ((), (), s32[]{:S(2)}) async-start(), calls=%async_computation.5 | async-start | bytes 3225600 | tf_op jit(solution)/shard_map/all_gather | solution.py:211
  8.7 2.7 copy-start.72
  8.7 2.9 copy-start.73
  8.7 3.2 copy-start.74
  8.7 3.4 copy-start.75
  8.7 24.8 %copy-start.71 = (s32[2]{0:T(128)S(1)}, s32[2]{0:T(128)}, u32[]{:S(2)}) copy-start(s32[2]{0:T(128)} %param.12) | copy-start | bytes 28
  8.7 26.7 %copy-start.11 = (bf16[2,128,1120]{1,2,0:T(8,128)(2,1)S(1)}, bf16[2,128,1120]{1,2,0:T(8,128)(2,1)}, u32[]{:S(2)}) copy-start(bf16[2,128,1120]{1,2,0:T(8,128)(2,1)} %param.11) | copy-start | bytes 1720324
  8.7 373.5 %all-gather.17.cloned.1.call-start = ((), (), s32[]{:S(2)}) async-start(), calls=%async_computation.6 | async-start | bytes 12544000 | tf_op jit(solution)/shard_map/all_gather | solution.py:214
  9.5 553.6 %all-gather.19.cloned.1.call-start = ((), (), s32[]{:S(2)}) async-start(), calls=%async_computation.7 | async-start | bytes 12902400 | tf_op jit(solution)/shard_map/all_gather | solution.py:215
  10.0 657.7 %reduce-scatter.15.cloned.1.call-start = ((), (), s32[]{:S(2)}) async-start(), calls=%async_computation.14 | async-start | bytes 3225600
  35.6 172.8 %copy-start.62 = (f32[128]{0:T(128)}, f32[128]{0:T(128)S(1)}, u32[]{:S(2)}) copy-start(f32[128]{0:T(128)S(1)} %get-tuple-element.76) | copy-start | bytes 1540
  35.6 567.3 %copy-start.55 = (f32[128]{0:T(128)}, f32[128]{0:T(128)S(1)}, u32[]{:S(2)}) copy-start(f32[128]{0:T(128)S(1)} %get-tuple-element.77) | copy-start | bytes 1540
  35.8 567.1 %copy-start.58 = (f32[128]{0:T(128)}, f32[128]{0:T(128)S(1)}, u32[]{:S(2)}) copy-start(f32[128]{0:T(128)S(1)} %add_rsqrt_fusion.3) | copy-start | bytes 1540
  35.8 172.6 %copy-start.66 = (f32[128]{0:T(128)}, f32[128]{0:T(128)S(1)}, u32[]{:S(2)}) copy-start(f32[128]{0:T(128)S(1)} %add_rsqrt_fusion.1) | copy-start | bytes 1540
  160.1 48.1 %copy-start.48 = (bf16[20,56,128]{2,1,0:T(8,128)(2,1)}, bf16[20,56,128]{2,1,0:T(8,128)(2,1)S(1)}, u32[]{:S(2)}) copy-start(bf16[20,56,128]{2,1,0:T(8,128)(2,1)S(1)} %convolution_convert_fusion.7) | copy-start | bytes 860164
  208.2 411.5 %copy-start.6 = (f32[128,1120]{0,1:T(8,128)}, f32[128,1120]{0,1:T(8,128)S(1)}, u32[]{:S(2)}) copy-start(f32[128,1120]{0,1:T(8,128)S(1)} %get-tuple-element.69) | copy-start | bytes 1720324
  215.9 2.2 copy-start.1
  215.9 2.3 copy-start.12
  216.5 3.8 copy-start.50
  563.1 9.2 copy-start
  576.9 8.2 copy-start.16
  576.9 8.2 copy-start.9
  577.0 8.2 copy-start.61
  585.1 4.0 copy-start.24
  593.4 186.3 %reduce-scatter.13.cloned.1.call-start = ((), (), s32[]{:S(2)}) async-start(), calls=%async_computation.13 | async-start | bytes 9676800
  593.5 2.0 copy-start.5
  593.5 2.0 copy-start.47
  597.5 13.2 copy-start.35
  597.9 12.9 copy-start.36
  601.7 9.0 copy-start.39
  602.3 8.4 copy-start.41
  602.9 7.8 copy-start.43
  603.0 7.8 copy-start.63
  603.0 7.8 copy-start.67
  619.6 10.2 copy-start.10
  619.6 349.0 %reduce-scatter.17.cloned.1.call-start = ((), (), s32[]{:S(2)}) async-start(), calls=%async_computation.15 | async-start | bytes 12544000
  641.6 508.0 %reduce-scatter.11.cloned.1.call-start = ((), (), s32[]{:S(2)}) async-start(), calls=%async_computation.8 | async-start | bytes 12902400 | tf_op jit(solution)/shard_map/reduce_scatter | solution.py:228
  667.7 550.3 %all-gather.23.cloned.1.call-start = ((), (), s32[]{:S(2)}) async-start(), calls=%async_computation.10 | async-start | bytes 5806080 | tf_op jit(solution)/shard_map/all_gather | solution.py:234
  668.4 611.3 %all-gather.21.cloned.1.call-start = ((), (), s32[]{:S(2)}) async-start(), calls=%async_computation.9 | async-start | bytes 17418240 | tf_op jit(solution)/shard_map/all_gather | solution.py:234
  779.7 605.6 %all-gather.25.cloned.1.call-start = ((), (), s32[]{:S(2)}) async-start(), calls=%async_computation.11 | async-start | bytes 22579200 | tf_op jit(solution)/shard_map/all_gather | solution.py:234
  968.6 190.1 %slice-start = ((s8[7741440]{0:T(1024)(128)(4,1)}), s8[3547136]{0:T(1024)(128)(4,1)S(1)}, s32[]{:S(2)}) async-start(s8[7741440]{0:T(1024)(128)(4,1)} %bitcast.188), calls=%async_computation.16 | async-start | bytes 7094272
  968.7 524.5 %all-gather.27.cloned.1.call-start = ((), (), s32[]{:S(2)}) async-start(), calls=%async_computation.12 | async-start | bytes 23224320 | tf_op jit(solution)/shard_map/all_gather | solution.py:234
  1153.0 5.7 slice-start.1
  1153.0 5.7 copy-start.14
  1153.0 5.8 copy-start.38
  1153.0 5.8 copy-start.40
  1153.0 5.8 copy-start.42
  1153.0 5.8 copy-start.56
  1153.0 5.8 copy-start.59
  1153.0 5.8 copy-start.64
  1153.0 5.8 copy-start.68
  1158.8 3.7 copy-start.52
  1198.0 9.4 copy-start.7
  1198.0 9.5 copy-start.18
  1207.4 9.2 copy-start.15
  1207.5 9.2 copy-start.21
  1207.5 9.2 copy-start.23
  1207.5 9.2 copy-start.53
  1207.5 9.1 copy-start.54
  1207.5 9.1 copy-start.57
  1207.5 9.1 copy-start.60
  1207.5 9.1 copy-start.65
  1207.5 9.1 copy-start.69
  (26 other events, 34.6 us)
Sparse Core Ops, SparseCore 0:
  9.6 141.9 all-gather.12
  153.1 52.2 all-gather.14
  206.9 175.2 all-gather.16
  383.7 179.3 all-gather.18
  593.5 49.2 reduce-scatter.14
  644.9 134.7 reduce-scatter.12
  782.1 186.5 reduce-scatter.16
  971.0 178.6 reduce-scatter.10
  1151.6 41.8 all-gather.22
  1195.2 84.4 all-gather.20
  1281.6 103.6 all-gather.24
  1387.0 106.0 all-gather.26
